TPU v7x, 256 devices: a whole 4x4x8 slice. The times are simulated.
256 devices in a mesh: grid: 64 (over x, z_lo, y), band: 4 (over z_hi, core).
Axes of the slice: x: 4, y: 4, z: 8 (z_hi: 2, z_lo: 4; z = z_hi * 4 + z_lo), core: 2. Of those that a mesh axis runs over, the one named last changes fastest.
Arguments:
- coefficients: float32 [2, 4, 1048576], P(None, 'band', 'grid'), may hold values from -60 to 60
- index_map: int32 [1048576], P('grid'), may hold values from 0 to 110591, as said below
- potential: float32 [192, 36864], P('grid'), may hold values from 0.5 to 2.5
Outputs:
- subspace: float32 [2, 4, 4], P(None, None, 'band')
- residual: float32 [2, 4, 1048576], P(None, 'band', 'grid')
Inputs may be any that keep to these rules, and one draw needn't show every extreme that they name: `index_map`: entries 16384 * g to 16384 * (g + 1) - 1 name distinct cells m = ga * 3 * 192 + (gb % 3) * 192 + gc of grid device g's slab of frequency planes, all with fa * fa + fc * fc < 2304, where fa and fc are ga and gc folded into -96 to 95.
All inputs are finite; a program needn't handle non-finite values.
Results may differ from a plain program's by a relative error of at most 0.000062.
Values sent between devices are 32-bit elements; how exact they have to be, the bound alone decides.
A program may use at most 64 MiB of HBM per device.

v0:
```python
import math

import jax
import jax.numpy as jnp
from jax import lax
from jax.sharding import PartitionSpec as P

N = 192


def make_tables(row_freq, width):
    column_pos = jnp.arange(width, dtype=jnp.int32)
    product = row_freq[:, None] * column_pos[None, :] % width
    angle = product.astype(jnp.float32) * (2.0 * math.pi / width)
    return (jnp.cos(angle), jnp.sin(angle))


def transform(spectrum, pattern, cos_table, sine_table, direction):
    highest = lax.Precision.HIGHEST
    real_part, imag_part = spectrum
    real_cos = jnp.einsum(pattern, real_part, cos_table, precision=highest)
    real_sin = jnp.einsum(pattern, real_part, sine_table, precision=highest)
    imag_cos = jnp.einsum(pattern, imag_part, cos_table, precision=highest)
    imag_sin = jnp.einsum(pattern, imag_part, sine_table, precision=highest)
    if direction > 0:
        return (real_cos - imag_sin, real_sin + imag_cos)
    return (real_cos + imag_sin, imag_cos - real_sin)


def local(coefficients, index_map, potential):
    width = N
    parts = lax.axis_size("grid")
    planes = potential.shape[0]
    band_count = coefficients.shape[1]
    coef_count = coefficients.shape[2]
    total_coef = coef_count * parts
    norm_factor = 1.0 / float(width) ** 3
    cos_full, sine_full = make_tables(jnp.arange(width, dtype=jnp.int32), width)
    weighted_pot = potential.reshape(planes, width, width) * norm_factor
    cell_total = width * planes * width
    real_part = (
        jnp.zeros((band_count, cell_total), jnp.float32).at[:, index_map].set(coefficients[0])
    )
    imag_part = (
        jnp.zeros((band_count, cell_total), jnp.float32).at[:, index_map].set(coefficients[1])
    )
    spectrum = (
        real_part.reshape(band_count, width, planes, width),
        imag_part.reshape(band_count, width, planes, width),
    )
    spectrum = transform(spectrum, "bpqc,cd->bpqd", cos_full, sine_full, 1)
    spectrum = transform(spectrum, "bapc,ad->bdpc", cos_full, sine_full, 1)
    moved = transform(
        (
            lax.all_to_all(spectrum[0], "grid", split_axis=1, concat_axis=2, tiled=True),
            lax.all_to_all(spectrum[1], "grid", split_axis=1, concat_axis=2, tiled=True),
        ),
        "bxgc,gd->bxdc",
        cos_full,
        sine_full,
        1,
    )
    moved = (moved[0] * weighted_pot[None], moved[1] * weighted_pot[None])
    moved = transform(moved, "bxgc,gd->bxdc", cos_full, sine_full, -1)
    spectrum = (
        lax.all_to_all(moved[0], "grid", split_axis=2, concat_axis=1, tiled=True),
        lax.all_to_all(moved[1], "grid", split_axis=2, concat_axis=1, tiled=True),
    )
    spectrum = transform(spectrum, "bapc,ad->bdpc", cos_full, sine_full, -1)
    spectrum = transform(spectrum, "bpqc,cd->bpqd", cos_full, sine_full, -1)
    applied_re = jnp.take(spectrum[0].reshape(band_count, cell_total), index_map, axis=1)
    applied_im = jnp.take(spectrum[1].reshape(band_count, cell_total), index_map, axis=1)
    all_coefs = lax.all_gather(coefficients, "band", axis=1, tiled=True)
    highest = lax.Precision.HIGHEST
    coef_re = all_coefs[0]
    coef_im = all_coefs[1]
    part_re = (
        jnp.dot(coef_re, applied_re.T, precision=highest)
        + jnp.dot(coef_im, applied_im.T, precision=highest)
    ) / total_coef
    part_im = (
        jnp.dot(coef_re, applied_im.T, precision=highest)
        - jnp.dot(coef_im, applied_re.T, precision=highest)
    ) / total_coef
    sub_re, sub_im = lax.psum((part_re, part_im), "grid")
    resid_re = applied_re - (
        jnp.dot(sub_re.T, coef_re, precision=highest)
        - jnp.dot(sub_im.T, coef_im, precision=highest)
    )
    resid_im = applied_im - (
        jnp.dot(sub_im.T, coef_re, precision=highest)
        + jnp.dot(sub_re.T, coef_im, precision=highest)
    )
    return (jnp.stack([sub_re, sub_im]), jnp.stack([resid_re, resid_im]))


def solution(mesh):
    return jax.shard_map(
        local,
        mesh=mesh,
        in_specs=(P(None, "band", "grid"), P("grid"), P("grid", None)),
        out_specs=(P(None, None, "band"), P(None, "band", "grid")),
        check_vma=False,
    )
```

profile of v0, /device:TPU:8, one launch (start us, length us, event | category | flops | bytes accessed | tf_op | source)
XLA Modules:
  0.0 645.2 jit_solution(5348410996851346691)
XLA Ops:
  1.6 60.5 %scatter_custom_fusion = f32[110592]{0:T(1024)S(1)} fusion(s32[16384]{0:T(1024)S(1)} %get-tuple-element.12, f32[16384]{0:T(1024)S(1)} %bitcast.225, f32[]{:T(128)} %constant.18.clone.1), kind=kCustom, calls=%fused_computation.58 | custom fusion | bytes 442372 | tf_op jit(solution)/shard_map/scatter | solution.py:42
  65.3 60.6 %scatter_custom_fusion.1 = f32[110592]{0:T(1024)S(1)} fusion(s32[16384]{0:T(1024)S(1)} %get-tuple-element.12, f32[16384]{0:T(1024)S(1)} %bitcast.224, f32[]{:T(128)} %constant.18.clone.1), kind=kCustom, calls=%fused_computation.56 | custom fusion | bytes 442372 | tf_op jit(solution)/shard_map/scatter | solution.py:45
  130.6 1.5 fusion.9
  132.0 1.4 copy.92
  133.5 12.0 %all-to-all-start = ((f32[1,192,3,192]{3,0,2,1:T(1,128)}), f32[1,192,3,192]{3,0,2,1:T(1,128)S(1)}, u32[]{:S(2)}, u32[]{:S(2)}) async-start(f32[1,192,3,192]{3,0,2,1:T(1,128)} %copy.92), calls=%async_computation | async-start | bytes 1179648 | tf_op jit(solution)/shard_map/all_to_all | solution.py:55
  145.5 1.4 fusion.46
  146.9 1.4 fusion.8
  148.3 1.4 copy.97
  149.8 14.4 %all-to-all-done = f32[1,192,3,192]{3,0,2,1:T(1,128)S(1)} async-done(((f32[1,192,3,192]{3,0,2,1:T(1,128)}), f32[1,192,3,192]{3,0,2,1:T(1,128)S(1)}, u32[]{:S(2)}, u32[]{:S(2)}) %all-to-all-start) | async-done | bytes 442400 | tf_op jit(solution)/shard_map/all_to_all | solution.py:55
  164.1 5.9 all-to-all-start.1
  171.1 1.4 fusion.43
  172.6 2.3 fusion.68
  174.8 13.3 %all-to-all-done.1 = f32[1,192,3,192]{3,0,2,1:T(1,128)S(1)} async-done(((f32[1,192,3,192]{3,0,2,1:T(1,128)}), f32[1,192,3,192]{3,0,2,1:T(1,128)S(1)}, u32[]{:S(2)}, u32[]{:S(2)}) %all-to-all-start.1) | async-done | bytes 442400 | tf_op jit(solution)/shard_map/all_to_all | solution.py:56
  190.5 1.4 fusion.4
  192.0 1.5 fusion.7
  193.4 1.4 fusion.56
  194.9 1.4 fusion
  196.3 1.4 copy.110
  197.7 6.0 all-to-all-start.3
  203.9 19.6 %all_gather.3 = f32[2,4,16384]{2,0,1:T(2,128)S(1)} all-gather(f32[2,1,16384]{2,0,1:T(2,128)S(1)} %copy.117), channel_id=1, replica_groups=mesh['grid'=64,'band'=4] {'band'}, dimensions={1}, use_global_device_ids=true | all-gather | bytes 655360 | tf_op jit(solution)/shard_map/all_gather | solution.py:73
  225.0 1.5 fusion.1
  226.4 1.4 copy.104
  227.9 10.8 %all-to-all-start.2 = ((f32[1,3,192,192]{3,0,1,2:T(1,128)}), f32[1,3,192,192]{3,0,1,2:T(1,128)S(1)}, u32[]{:S(2)}, u32[]{:S(2)}) async-start(f32[1,3,192,192]{3,0,1,2:T(1,128)} %copy.104), calls=%async_computation.2 | async-start | bytes 1179648 | tf_op jit(solution)/shard_map/all_to_all | solution.py:66
  240.2 17.5 %all-to-all-done.2 = f32[1,3,192,192]{3,0,1,2:T(1,128)S(1)} async-done(((f32[1,3,192,192]{3,0,1,2:T(1,128)}), f32[1,3,192,192]{3,0,1,2:T(1,128)S(1)}, u32[]{:S(2)}, u32[]{:S(2)}) %all-to-all-start.2) | async-done | bytes 442400 | tf_op jit(solution)/shard_map/all_to_all | solution.py:66
  258.8 1.4 fusion.72
  260.3 1.4 fusion.54
  261.7 1.4 convolution_add_fusion.1
  263.1 1.4 convolution_subtract_fusion.1
  267.4 1.6 convolution_subtract_fusion
  272.2 90.5 %gather_fusion = f32[16384]{0:T(1024)S(1)} fusion(f32[110592]{0:T(1024)S(1)} %reshape.245, s32[16384]{0:T(1024)S(1)} %get-tuple-element.11), kind=kCustom, calls=%fused_computation.clone | custom fusion | bytes 196608 | tf_op jit(solution)/shard_map/jit(_take)/gather | solution.py:71
  362.7 90.5 %gather_fusion.1 = f32[16384]{0:T(1024)S(1)} fusion(f32[110592]{0:T(1024)S(1)} %reshape.248, s32[16384]{0:T(1024)S(1)} %get-tuple-element.11), kind=kCustom, calls=%fused_computation.1.clone | custom fusion | bytes 196608 | tf_op jit(solution)/shard_map/jit(_take)/gather | solution.py:72
  458.1 182.6 %all-reduce = (f32[4,1]{0,1:T(1,128)S(1)}, f32[4,1]{0,1:T(1,128)S(1)}) all-reduce(f32[4,1]{0,1:T(1,128)S(1)} %fusion.15, f32[4,1]{0,1:T(1,128)S(1)} %fusion.12), channel_id=1, replica_groups=mesh['grid'=64,'band'=4] {'grid'}, use_global_device_ids=true, to_apply=%region_3.5 | all-reduce | flops 8 | bytes 64 | tf_op jit(solution)/shard_map/psum | solution.py:85
  (57 shorter events, 31.4 us)
Async XLA Ops:
  0.6 0.9 copy-start.4
  133.5 30.7 %all-to-all-start = ((f32[1,192,3,192]{3,0,2,1:T(1,128)}), f32[1,192,3,192]{3,0,2,1:T(1,128)S(1)}, u32[]{:S(2)}, u32[]{:S(2)}) async-start(f32[1,192,3,192]{3,0,2,1:T(1,128)} %copy.92), calls=%async_computation | async-start | bytes 1179648 | tf_op jit(solution)/shard_map/all_to_all | solution.py:55
  149.8 20.3 %copy-start.2 = (f32[3,36864]{1,0:T(4,128)S(1)}, f32[3,36864]{1,0:T(4,128)}, u32[]{:S(2)}) copy-start(f32[3,36864]{1,0:T(4,128)} %param.7) | copy-start | bytes 1327108
  164.1 24.0 %all-to-all-start.1 = ((f32[1,192,3,192]{3,0,2,1:T(1,128)}), f32[1,192,3,192]{3,0,2,1:T(1,128)S(1)}, u32[]{:S(2)}, u32[]{:S(2)}) async-start(f32[1,192,3,192]{3,0,2,1:T(1,128)} %copy.97), calls=%async_computation.1 | async-start | bytes 1179648 | tf_op jit(solution)/shard_map/all_to_all | solution.py:56
  188.1 0.8 copy-start
  190.5 1.4 copy-start.1
  197.7 6.0 copy-start.3
  197.7 30.1 %all-to-all-start.3 = ((f32[1,3,192,192]{3,0,1,2:T(1,128)}), f32[1,3,192,192]{3,0,1,2:T(1,128)S(1)}, u32[]{:S(2)}, u32[]{:S(2)}) async-start(f32[1,3,192,192]{3,0,1,2:T(1,128)} %copy.110), calls=%async_computation.3 | async-start | bytes 1179648 | tf_op jit(solution)/shard_map/all_to_all | solution.py:67
  227.9 29.8 %all-to-all-start.2 = ((f32[1,3,192,192]{3,0,1,2:T(1,128)}), f32[1,3,192,192]{3,0,1,2:T(1,128)S(1)}, u32[]{:S(2)}, u32[]{:S(2)}) async-start(f32[1,3,192,192]{3,0,1,2:T(1,128)} %copy.104), calls=%async_computation.2 | async-start | bytes 1179648 | tf_op jit(solution)/shard_map/all_to_all | solution.py:66
where the time goes:
time: 650 us; the launch traced here: 645 us
  local copies, waits for them, and re-layouts  317 us (49%)
  blocking collectives  202 us (31%)
  waiting for transfers between devices  45.1 us (7%)
  matrix products  42.7 us (7%)
  starting transfers between devices  34.8 us (5%)
    psum x1, blocking collectives, local(): sub_re, sub_im = lax.psum((part_re, part_im), 'grid')  183 us
    scatter x2, local copies, waits for them, and re-layouts, local(): jnp.zeros((band_count, cell_total), jnp.float32).at[:, index_map]  121 us
    gather x1, local copies, waits for them, and re-layouts, local(): jnp.take(spectrum[0].reshape(band_count, cell_total), index_map, axis=1)  90.5 us
    gather x1, local copies, waits for them, and re-layouts, local(): jnp.take(spectrum[1].reshape(band_count, cell_total), index_map, axis=1)  90.5 us
    all_gather x1, blocking collectives, local(): all_coefs = lax.all_gather(coefficients, 'band', axis=1, tiled=True)  19.6 us
    all_to_all x1, waiting for transfers between devices, local(): lax.all_to_all(moved[0], 'grid', split_axis=2, concat_axis=1, tiled=True)  17.5 us
    all_to_all x1, waiting for transfers between devices, local(): lax.all_to_all(spectrum[0], 'grid', split_axis=1, concat_axis=2, tiled=True)  14.4 us
    all_to_all x1, waiting for transfers between devices, local(): lax.all_to_all(spectrum[1], 'grid', split_axis=1, concat_axis=2, tiled=True)  13.3 us
  transfers between devices with their start and end apart: 4, of which 3 were waited for; matrix products, arithmetic and copies ran while one was open for 2% of the time, Pallas kernels for 0%

commit v1 on v0

v1 whole, which is shorter than its diff:
```python
import functools
import math

import jax
import jax.numpy as jnp
import ml_dtypes
import numpy as np
from jax import lax
from jax.experimental import pallas as pl
from jax.experimental.pallas import tpu as pltpu
from jax.sharding import PartitionSpec as P

N = 192
HALF = 96
PARTS = 64
SLAB = 3
KS = 8
LA, LB = 384, 256
LANES = LA + LB
F32, BF16 = jnp.float32, jnp.bfloat16
MESH = pl.DeviceIdType.MESH
VMEM = pltpu.VMEM


def split(table):
    hi = table.astype(np.float32).astype(ml_dtypes.bfloat16)
    lo = (table - hi.astype(np.float64)).astype(np.float32).astype(ml_dtypes.bfloat16)
    return hi, lo


def make_tables():
    turn = 2.0 * math.pi / N
    fold = np.arange(HALF)
    freq = np.where(fold < HALF // 2, fold, fold + HALF)
    plane = 3 * np.arange(PARTS)[None, :] + np.arange(SLAB)[:, None]
    plane = plane.reshape(-1)
    cells = np.arange(N)
    angle = turn * (plane[:, None] * freq[None, :] % N)
    first = np.concatenate([np.cos(angle), np.sin(angle)], 0)
    angle = turn * (cells[:, None] * plane[None, :] % N)
    middle = np.concatenate([np.cos(angle), np.sin(angle)], 0)
    lane_freq = np.zeros(256, np.int64)
    kind = np.full(256, -1)
    lane_freq[0:64], kind[0:64] = freq[:64], 0
    lane_freq[64:128], kind[64:128] = freq[:64], 1
    lane_freq[128:160], kind[128:160] = freq[64:], 0
    lane_freq[192:224], kind[192:224] = freq[64:], 1
    angle = turn * (lane_freq[:, None] * cells[None, :] % N)
    cos, sin = np.cos(angle), np.sin(angle)
    re, im = (kind == 0)[:, None], (kind == 1)[:, None]
    to_re = re * cos - im * sin
    to_im = re * sin + im * cos
    norm = 1.0 / float(N) ** 3
    from_re = (re * cos - im * sin).T * norm
    from_im = (re * sin + im * cos).T * norm
    angle = turn * (plane[:, None] * cells[None, :] % N)
    middle_back = np.concatenate([np.cos(angle), np.sin(angle)], 0)
    angle = turn * (freq[:, None] * plane[None, :] % N)
    first_back = np.concatenate([np.cos(angle), np.sin(angle)], 0)
    tables = (first, middle, to_re, to_im, from_re, from_im, middle_back, first_back)
    return [np.stack(split(table)) for table in tables]


def halves(x):
    hi = x.astype(BF16)
    return hi, (x - hi.astype(F32)).astype(BF16)


def dot(a, b):
    return jnp.dot(a, b, preferred_element_type=F32)


def dot_left(table, hi, lo):
    return dot(table[0], hi) + dot(table[1], hi) + dot(table[0], lo)


def dot_right(hi, lo, table):
    return dot(hi, table[0]) + dot(lo, table[0]) + dot(hi, table[1])


def groups(x):
    return [x[:, 128 * g : 128 * g + 128] for g in range(x.shape[1] // 128)]


def combine(both, sign):
    rows = both.shape[0] // 2
    lane = lax.broadcasted_iota(jnp.int32, (rows, 128), 1)
    factor = jnp.where(lane < 64, -sign, sign).astype(F32)
    parts = [
        c + factor * pltpu.roll(s, 64, 1)
        for c, s in zip(groups(both[:rows]), groups(both[rows:]))
    ]
    return jnp.concatenate(parts, 1)


def kernel(
    index_ref,
    coef_ref,
    pot_ref,
    first,
    middle,
    to_re,
    to_im,
    from_re,
    from_im,
    middle_back,
    first_back,
    sub_ref,
    res_ref,
    row_key,
    col_key,
    coef_hi,
    coef_lo,
    acc,
    send1,
    recv1,
    send2,
    recv2,
    trash,
    table,
    all_coef,
    applied,
    part,
    parts_in,
    send_sem,
    recv_sem,
    band_send,
    band_recv,
    own_sem,
):
    me = lax.axis_index("grid")
    band = lax.axis_index("band")
    sibling = band + 1 - 2 * lax.rem(band, 2)
    across = lax.rem(band + 2, 4)
    opposite = lax.rem(sibling + 2, 4)

    barrier = pltpu.get_barrier_semaphore()

    def greet(i, carry):
        peer = lax.rem(me + i, PARTS)
        pl.semaphore_signal(barrier, inc=1, device_id={"grid": peer}, device_id_type=MESH)
        return carry

    lax.fori_loop(1, PARTS, greet, 0)
    pl.semaphore_signal(barrier, inc=1, device_id={"band": sibling}, device_id_type=MESH)
    pl.semaphore_signal(barrier, inc=1, device_id={"band": across}, device_id_type=MESH)

    cell = index_ref[...].astype(F32)
    line = jnp.floor((cell + 0.5) * (1.0 / N))
    gc = cell - N * line
    ga = jnp.floor((cell + 0.5) * (1.0 / (SLAB * N)))
    slab = line - SLAB * ga
    row_key[...] = slab * HALF + jnp.where(ga < HALF, ga, ga - HALF)
    col_key[...] = jnp.where(gc < HALF, gc, gc - HALF)
    coef = coef_ref[...]
    coef_hi[...] = coef.astype(BF16).astype(F32)
    coef_lo[...] = coef - coef.astype(BF16).astype(F32)
    acc[...] = jnp.zeros_like(acc)

    iota96 = lax.broadcasted_iota(jnp.int32, (HALF, 128), 0).astype(F32)
    iota96h = iota96.astype(BF16)
    one, zero = jnp.ones((), BF16), jnp.zeros((), BF16)
    zero32 = jnp.zeros((32, 128), BF16)

    def wide(x):
        return jnp.broadcast_to(x.astype(BF16), (HALF, 128))

    def row_hot(i):
        pieces = []
        for s in range(KS):
            key = row_key[pl.ds(i * KS + s, 1), :]
            pieces.append(
                jnp.concatenate(
                    [jnp.where(iota96h == wide(key - HALF * p), one, zero) for p in range(SLAB)], 0
                )
            )
        return jnp.concatenate(pieces, 1)

    def scatter_step(i, carry):
        pieces = []
        for s in range(KS):
            row = pl.ds(i * KS + s, 1)
            mask = iota96h == wide(col_key[row, :])
            blocks = []
            for ref in (coef_hi, coef_lo):
                re = jnp.where(mask, wide(ref[0, row, :]), zero)
                im = jnp.where(mask, wide(ref[1, row, :]), zero)
                blocks += [re[:64], im[:64], re[64:], zero32, im[64:], zero32]
            pieces.append(jnp.concatenate(blocks, 0))
        acc[...] += lax.dot_general(
            row_hot(i),
            jnp.concatenate(pieces, 1),
            (((1,), (1,)), ((), ())),
            preferred_element_type=F32,
        )
        return carry

    steps = 128 // KS
    lax.fori_loop(0, 4, scatter_step, 0)
    pl.semaphore_wait(barrier, PARTS - 1 + 2)

    def band_copy(src, dst, slot, to):
        return pltpu.make_async_remote_copy(
            src_ref=src,
            dst_ref=dst,
            send_sem=band_send.at[slot],
            recv_sem=band_recv.at[slot],
            device_id={"band": to},
            device_id_type=MESH,
        )

    to_across = band_copy(coef_ref, all_coef.at[band], 0, across)
    to_sibling = band_copy(coef_ref, all_coef.at[band], 1, sibling)
    keep = pltpu.make_async_copy(coef_ref, all_coef.at[band], own_sem)
    to_across.start()
    to_sibling.start()
    keep.start()
    lax.fori_loop(4, steps, scatter_step, 0)

    def exchange(src, dst, lanes, slot):
        def one_copy(i, carry):
            peer = lax.rem(me + i, PARTS)
            pltpu.make_async_remote_copy(
                src_ref=src.at[:, peer, lanes],
                dst_ref=dst.at[:, me, lanes],
                send_sem=send_sem.at[slot],
                recv_sem=recv_sem.at[slot],
                device_id={"grid": peer},
                device_id_type=MESH,
            ).start()
            return carry

        lax.fori_loop(1, PARTS, one_copy, 0)
        pltpu.make_async_copy(src.at[:, me, lanes], dst.at[:, me, lanes], recv_sem.at[slot]).start()
        pltpu.make_async_copy(
            src.at[:, me, lanes], trash.at[slot, :, 0, lanes], send_sem.at[slot]
        ).start()

    def arrive(src, dst, lanes, slot):
        pltpu.make_async_copy(src.at[:, :, lanes], dst.at[:, :, lanes], recv_sem.at[slot]).wait()

    def sent(src, dst, lanes, slot):
        pltpu.make_async_copy(src.at[:, :, lanes], dst.at[:, :, lanes], send_sem.at[slot]).wait()

    lanes_a, lanes_b = pl.ds(0, LA), pl.ds(LA, LB)

    def spectrum(offset):
        a = [acc[HALF * p : HALF * p + HALF, offset : offset + 128] for p in range(SLAB)]
        b = [acc[HALF * p : HALF * p + HALF, offset + 128 : offset + 256] for p in range(SLAB)]
        return (
            jnp.concatenate(a, 1).astype(BF16),
            jnp.concatenate([b[0] + pltpu.roll(b[1], 32, 1), b[2]], 1).astype(BF16),
        )

    hi_a, hi_b = spectrum(0)
    lo_a, lo_b = spectrum(256)
    out_a = combine(dot_left(first, hi_a, lo_a), 1.0)
    for j in range(SLAB):
        send1[j, :, 0:LA] = out_a[PARTS * j : PARTS * j + PARTS]
    exchange(send1, recv1, lanes_a, 0)
    out_b = combine(dot_left(first, hi_b, lo_b), 1.0)
    for j in range(SLAB):
        send1[j, :, LA:LANES] = out_b[PARTS * j : PARTS * j + PARTS]
    exchange(send1, recv1, lanes_b, 1)

    band_copy(coef_ref, all_coef.at[across], 0, across).wait_recv()
    onward = band_copy(all_coef.at[across], all_coef.at[across], 2, sibling)
    onward.start()

    arrive(send1, recv1, lanes_a, 0)
    arrive(send1, recv1, lanes_b, 1)

    def middle_step(j, carry):
        x = recv1[j]
        a = jnp.concatenate([x[:, 0:128], x[:, 128:256], x[:, 256:384]], 0)
        b = jnp.concatenate([x[:, 384:512], pltpu.roll(x[:, 384:512], 96, 1), x[:, 512:640]], 0)
        x = combine(dot_left(middle, *halves(jnp.concatenate([a, b], 1))), 1.0)
        hi, lo = halves(x)
        pot = pot_ref[j]
        field_re = dot_right(hi, lo, to_re) * pot
        field_im = dot_right(hi, lo, to_im) * pot
        x = dot_right(*halves(field_re), from_re) + dot_right(*halves(field_im), from_im)
        x = combine(dot_left(middle_back, *halves(x)), -1.0)
        for p in range(SLAB):
            send2[j, :, 128 * p : 128 * p + 128] = x[PARTS * p : PARTS * p + PARTS, 0:128]
        send2[j, :, 384:512] = x[0:64, 128:256] + pltpu.roll(x[64:128, 128:256], 32, 1)
        send2[j, :, 512:640] = x[128:192, 128:256]
        return carry

    lax.fori_loop(0, SLAB, middle_step, 0)
    exchange(send2, recv2, lanes_a, 2)
    exchange(send2, recv2, lanes_b, 3)
    arrive(send2, recv2, lanes_a, 2)
    arrive(send2, recv2, lanes_b, 3)

    x = recv2[...].reshape(N, LANES)
    x = combine(dot_left(first_back, *halves(x)), -1.0)
    b0 = x[:, 384:512]
    x = jnp.concatenate(
        [
            jnp.concatenate([x[:, 0:128], x[:, 128:256], x[:, 256:384]], 0),
            jnp.concatenate([b0, pltpu.roll(b0, 96, 1), x[:, 512:640]], 0),
        ],
        1,
    ).T
    x = jnp.concatenate([x[0:64], x[128:160], x[64:128], x[192:224]], 0)
    hi, lo = halves(x)
    table[0] = hi
    table[1] = lo

    def gather_step(i, carry):
        hot = row_hot(i)
        found = dot(table[0], hot) + dot(table[1], hot)
        for s in range(KS):
            row = pl.ds(i * KS + s, 1)
            mask = iota96 == jnp.broadcast_to(col_key[row, :], (HALF, 128))
            here = found[:, 128 * s : 128 * s + 128]
            for k in range(2):
                kept = jnp.where(mask, here[HALF * k : HALF * k + HALF], 0.0)
                applied[k, row, :] = kept.reshape(12, 8, 128).sum(0).sum(0, keepdims=True)
        return carry

    lax.fori_loop(0, steps, gather_step, 0)

    band_copy(coef_ref, all_coef.at[sibling], 1, sibling).wait_recv()
    band_copy(coef_ref, all_coef.at[opposite], 2, sibling).wait_recv()
    keep.wait()

    h_re, h_im = applied[0], applied[1]
    sums = []
    for i in range(4):
        c_re, c_im = all_coef[i, 0], all_coef[i, 1]
        sums.append((c_re * h_re + c_im * h_im, c_re * h_im - c_im * h_re))
    lanes = [s[0].sum(0, keepdims=True) for s in sums] + [s[1].sum(0, keepdims=True) for s in sums]
    total = jnp.concatenate(lanes, 0).sum(1, keepdims=True)
    eye = lax.broadcasted_iota(jnp.int32, (8, 128), 0) == lax.broadcasted_iota(
        jnp.int32, (8, 128), 1
    )
    line = jnp.where(eye, jnp.broadcast_to(total, (8, 128)), 0.0).sum(0, keepdims=True)
    part[...] = jnp.broadcast_to(line.reshape(1, 1, 128), part.shape)

    def share(i, carry):
        peer = lax.rem(me + i, PARTS)
        pltpu.make_async_remote_copy(
            src_ref=part.at[:, 0],
            dst_ref=parts_in.at[:, me],
            send_sem=send_sem.at[4],
            recv_sem=recv_sem.at[4],
            device_id={"grid": peer},
            device_id_type=MESH,
        ).start()
        return carry

    lax.fori_loop(1, PARTS, share, 0)
    pltpu.make_async_copy(part.at[:, 0], parts_in.at[:, me], recv_sem.at[4]).start()
    pltpu.make_async_copy(part.at[:, 0], trash.at[4, pl.ds(0, 1), 0, pl.ds(0, 128)], send_sem.at[4]).start()
    pltpu.make_async_copy(part, parts_in, recv_sem.at[4]).wait()

    line = parts_in[0].sum(0, keepdims=True) * (1.0 / (PARTS * 16384))
    sub_ref[...] = jnp.broadcast_to(line, (8, 128))
    r_re, r_im = h_re, h_im
    for i in range(4):
        s_re = jnp.broadcast_to(line[:, i : i + 1], (128, 128))
        s_im = jnp.broadcast_to(line[:, i + 4 : i + 5], (128, 128))
        c_re, c_im = all_coef[i, 0], all_coef[i, 1]
        r_re = r_re - (c_re * s_re - c_im * s_im)
        r_im = r_im - (c_re * s_im + c_im * s_re)
    res_ref[0] = r_re
    res_ref[1] = r_im

    sent(send1, recv1, lanes_a, 0)
    sent(send1, recv1, lanes_b, 1)
    sent(send2, recv2, lanes_a, 2)
    sent(send2, recv2, lanes_b, 3)
    pltpu.make_async_copy(part, parts_in, send_sem.at[4]).wait()
    to_across.wait_send()
    to_sibling.wait_send()
    onward.wait_send()


def local(coefficients, index_map, potential):
    tables = [jnp.asarray(t) for t in make_tables()]
    coef = coefficients.reshape(2, 128, 128)
    index = index_map.reshape(128, 128)
    pot = potential.reshape(SLAB, N, N)
    field = VMEM((SLAB, PARTS, LANES), F32)
    sub, res = pl.pallas_call(
        kernel,
        out_shape=(
            jax.ShapeDtypeStruct((8, 128), F32),
            jax.ShapeDtypeStruct((2, 128, 128), F32),
        ),
        in_specs=[pl.BlockSpec(memory_space=VMEM)] * (3 + len(tables)),
        out_specs=[pl.BlockSpec(memory_space=VMEM)] * 2,
        scratch_shapes=[
            VMEM((128, 128), F32),
            VMEM((128, 128), F32),
            VMEM((2, 128, 128), F32),
            VMEM((2, 128, 128), F32),
            VMEM((SLAB * HALF, 512), F32),
            field,
            field,
            field,
            field,
            VMEM((5, SLAB, 1, LANES), F32),
            VMEM((2, N, SLAB * HALF), BF16),
            VMEM((4, 2, 128, 128), F32),
            VMEM((2, 128, 128), F32),
            VMEM((1, PARTS, 128), F32),
            VMEM((1, PARTS, 128), F32),
            pltpu.SemaphoreType.DMA((5,)),
            pltpu.SemaphoreType.DMA((5,)),
            pltpu.SemaphoreType.DMA((3,)),
            pltpu.SemaphoreType.DMA((3,)),
            pltpu.SemaphoreType.DMA,
        ],
        compiler_params=pltpu.CompilerParams(
            collective_id=0, has_side_effects=True, vmem_limit_bytes=48 << 20
        ),
        name="apply_potential",
    )(index, coef, pot, *tables)
    return sub[0, :8].reshape(2, 4, 1), res.reshape(2, 1, 16384)


def solution(mesh):
    return jax.shard_map(
        local,
        mesh=mesh,
        in_specs=(P(None, "band", "grid"), P("grid"), P("grid", None)),
        out_specs=(P(None, None, "band"), P(None, "band", "grid")),
        check_vma=False,
    )
```

time: 650 us -> 75.3 us (0.12)
  local copies, waits for them, and re-layouts: 317 us -> 8.35 us
  blocking collectives: 202 us -> 0 us
  Pallas kernels: 0 us -> 65.8 us
  waiting for transfers between devices: 45.1 us -> 0 us
  matrix products: 42.7 us -> 0 us
  starting transfers between devices: 34.8 us -> 0 us
    psum x1 -> x0, blocking collectives: 183 us -> none  [local(): sub_re, sub_im = lax.psum((part_re, part_im), 'grid')]
    gather x2 -> x0, local copies, waits for them, and re-layouts: 181 us -> none  [the longest x1 90.5 us: local(): jnp.take(spectrum[0].reshape(band_count, cell_total), index_map, axis=1)]
    scatter x2 -> x0, local copies, waits for them, and re-layouts: 121 us -> none  [local(): jnp.zeros((band_count, cell_total), jnp.float32).at[:, index_map]]
    pallas_call x0 -> x1, Pallas kernels: none -> 65.8 us  [local(): pl.pallas_call(kernel, out_shape=(jax.ShapeDtypeStruct((8, 128), F32), ja...]
    all_to_all x4 -> x0, waiting for transfers between devices: 45.1 us -> none  [the longest x1 17.5 us: local(): lax.all_to_all(moved[0], 'grid', split_axis=2, concat_axis=1, tiled=True)]
    dot_general x32 -> x0, matrix products: 42.7 us -> none  [the longest x6 9.29 us: transform(): real_cos = jnp.einsum(pattern, real_part, cos_table, precision=highest)]
    all_to_all x4 -> x0, starting transfers between devices: 34.8 us -> none  [the longest x1 12 us: local(): lax.all_to_all(spectrum[0], 'grid', split_axis=1, concat_axis=2, tiled=True)]
    all_gather x1 -> x0, blocking collectives: 19.6 us -> none  [local(): all_coefs = lax.all_gather(coefficients, 'band', axis=1, tiled=True)]
  transfers between devices with their start and end apart: 4 -> 0, of which waited for: 3 -> 0; matrix products, arithmetic and copies ran while one was open for 2% -> 0% of each run, Pallas kernels for 0% -> 0%
where the time goes in v1:
time: 75.3 us; the launch traced here: 74.9 us
  Pallas kernels  65.8 us (87%)
  local copies, waits for them, and re-layouts  8.35 us (11%)
    pallas_call x1, Pallas kernels, local(): pl.pallas_call(kernel, out_shape=(jax.ShapeDtypeStruct((8, 128), F32), ja...  65.8 us
    unnamed x21, local copies, waits for them, and re-layouts  6.17 us
    reshape x1, local copies, waits for them, and re-layouts, local(): pot = potential.reshape(SLAB, N, N)  1.51 us

profile of v1, /device:TPU:8, one launch (start us, length us, event | category | flops | bytes accessed | tf_op | source)
XLA Modules:
  0.0 74.9 jit_solution(12376547849837193655)
XLA Ops:
  0.6 0.0 copy-start
  0.6 0.0 copy-start.1
  0.7 0.0 copy-start.2
  0.7 0.0 copy-start.8
  0.7 1.5 %reshape.18.pot_ref = f32[3,192,192]{2,1,0:T(8,128)S(1)} reshape(f32[3,36864]{1,0:T(4,128)} %param.13) | data formatting | bytes 884736 | tf_op jit(solution)/shard_map/reshape | solution.py:385
  2.2 0.0 copy-done
  2.2 0.0 copy-done.1
  2.2 0.0 copy-done.2
  2.2 0.0 copy-done.8
  2.2 0.0 copy-start.3
  2.2 0.9 %copy-done.3 = bf16[2,256,192]{2,1,0:T(8,128)(2,1)S(1)} copy-done((bf16[2,256,192]{2,1,0:T(8,128)(2,1)S(1)}, bf16[2,256,192]{2,1,0:T(8,128)(2,1)}, u32[]{:S(2)}) %copy-start.3) | copy-done | bytes 196632
  3.2 0.0 copy-start.4
  3.2 0.9 %copy-done.4 = bf16[2,192,192]{2,1,0:T(8,128)(2,1)S(1)} copy-done((bf16[2,192,192]{2,1,0:T(8,128)(2,1)S(1)}, bf16[2,192,192]{2,1,0:T(8,128)(2,1)}, u32[]{:S(2)}) %copy-start.4) | copy-done | bytes 147480
  4.1 0.0 copy-start.5
  4.1 0.9 %copy-done.5 = bf16[2,192,256]{2,1,0:T(8,128)(2,1)S(1)} copy-done((bf16[2,192,256]{2,1,0:T(8,128)(2,1)S(1)}, bf16[2,192,256]{2,1,0:T(8,128)(2,1)}, u32[]{:S(2)}) %copy-start.5) | copy-done | bytes 196632
  5.0 0.0 copy-start.6
  5.0 0.9 %copy-done.6 = bf16[2,192,256]{2,1,0:T(8,128)(2,1)S(1)} copy-done((bf16[2,192,256]{2,1,0:T(8,128)(2,1)S(1)}, bf16[2,192,256]{2,1,0:T(8,128)(2,1)}, u32[]{:S(2)}) %copy-start.6) | copy-done | bytes 196632
  6.0 0.0 copy-start.7
  6.0 0.9 %copy-done.7 = bf16[2,384,96]{2,1,0:T(8,128)(2,1)S(1)} copy-done((bf16[2,384,96]{2,1,0:T(8,128)(2,1)S(1)}, bf16[2,384,96]{2,1,0:T(8,128)(2,1)}, u32[]{:S(2)}) %copy-start.7) | copy-done | bytes 147480
  6.9 0.0 copy-start.9
  6.9 0.8 %copy-done.9 = s32[16384]{0:T(1024)S(1)} copy-done((s32[16384]{0:T(1024)S(1)}, s32[16384]{0:T(1024)}, u32[]{:S(2)}) %copy-start.9) | copy-done | bytes 65560
  7.7 65.8 %apply_potential.1 = (f32[8,128]{1,0:T(8,128)S(1)}, f32[2,128,128]{2,1,0:T(8,128)S(1)}) custom-call(s32[128,128]{1,0:T(8,128)S(1)} %bitcast.6, f32[2,128,128]{2,1,0:T(8,128)S(1)} %bitcast.4, f32[3,192,192]{2,1,0:T(8,128)S(1)} %reshape.18.pot_ref, bf16[2,384,96]{2,1,0:T(8,128)(2,1)S(1)} %copy-done.7, bf16[2,384,192]{2,1,0:T(8,128)(2,1)S(1)} %copy-done.1, ...), custom_call_target="tpu_custom_call" | custom-call | tf_op jit(solution)/shard_map/apply_potential/pallas_call | solution.py:387
  73.6 0.6 reshape_squeeze.3
  74.2 0.7 copy.16
  (1 shorter events, 0.0 us)
Async XLA Ops:
  0.6 1.6 %copy-start = (bf16[2,384,192]{2,1,0:T(8,128)(2,1)S(1)}, bf16[2,384,192]{2,1,0:T(8,128)(2,1)}, u32[]{:S(2)}) copy-start(bf16[2,384,192]{2,1,0:T(8,128)(2,1)} %constant.22.clone.middle_back) | copy-start | bytes 884740
  0.6 1.6 %copy-start.1 = (bf16[2,384,192]{2,1,0:T(8,128)(2,1)S(1)}, bf16[2,384,192]{2,1,0:T(8,128)(2,1)}, u32[]{:S(2)}) copy-start(bf16[2,384,192]{2,1,0:T(8,128)(2,1)} %constant.17.clone.middle) | copy-start | bytes 884740
  0.7 1.6 %copy-start.2 = (bf16[2,256,192]{2,1,0:T(8,128)(2,1)S(1)}, bf16[2,256,192]{2,1,0:T(8,128)(2,1)}, u32[]{:S(2)}) copy-start(bf16[2,256,192]{2,1,0:T(8,128)(2,1)} %constant.19.clone.to_im) | copy-start | bytes 589828
  0.7 1.6 %copy-start.8 = (f32[2,1,16384]{2,1,0:T(1,128)S(1)}, f32[2,1,16384]{2,1,0:T(1,128)}, u32[]{:S(2)}) copy-start(f32[2,1,16384]{2,1,0:T(1,128)} %param.11) | copy-start | bytes 393220
  2.2 1.0 %copy-start.3 = (bf16[2,256,192]{2,1,0:T(8,128)(2,1)S(1)}, bf16[2,256,192]{2,1,0:T(8,128)(2,1)}, u32[]{:S(2)}) copy-start(bf16[2,256,192]{2,1,0:T(8,128)(2,1)} %constant.18.clone.to_re) | copy-start | bytes 589828
  3.2 0.9 %copy-start.4 = (bf16[2,192,192]{2,1,0:T(8,128)(2,1)S(1)}, bf16[2,192,192]{2,1,0:T(8,128)(2,1)}, u32[]{:S(2)}) copy-start(bf16[2,192,192]{2,1,0:T(8,128)(2,1)} %constant.23.clone.first_back) | copy-start | bytes 442372
  4.1 0.9 %copy-start.5 = (bf16[2,192,256]{2,1,0:T(8,128)(2,1)S(1)}, bf16[2,192,256]{2,1,0:T(8,128)(2,1)}, u32[]{:S(2)}) copy-start(bf16[2,192,256]{2,1,0:T(8,128)(2,1)} %constant.21.clone.from_im) | copy-start | bytes 589828
  5.0 0.9 %copy-start.6 = (bf16[2,192,256]{2,1,0:T(8,128)(2,1)S(1)}, bf16[2,192,256]{2,1,0:T(8,128)(2,1)}, u32[]{:S(2)}) copy-start(bf16[2,192,256]{2,1,0:T(8,128)(2,1)} %constant.20.clone.from_re) | copy-start | bytes 589828
  6.0 0.9 %copy-start.7 = (bf16[2,384,96]{2,1,0:T(8,128)(2,1)S(1)}, bf16[2,384,96]{2,1,0:T(8,128)(2,1)}, u32[]{:S(2)}) copy-start(bf16[2,384,96]{2,1,0:T(8,128)(2,1)} %constant.16.clone.first) | copy-start | bytes 442372
  6.9 0.8 %copy-start.9 = (s32[16384]{0:T(1024)S(1)}, s32[16384]{0:T(1024)}, u32[]{:S(2)}) copy-start(s32[16384]{0:T(1024)} %param.12) | copy-start | bytes 196612

commit v2 on v1

--- a/solution.py
+++ b/solution.py
@@ -14,7 +14,7 @@
 HALF = 96
 PARTS = 64
 SLAB = 3
-KS = 8
+KS = 16
 LA, LB = 384, 256
 LANES = LA + LB
 F32, BF16 = jnp.float32, jnp.bfloat16
@@ -35,9 +35,10 @@
     plane = 3 * np.arange(PARTS)[None, :] + np.arange(SLAB)[:, None]
     plane = plane.reshape(-1)
     cells = np.arange(N)
+    paired = np.concatenate([cells[0::2], cells[1::2]])
     angle = turn * (plane[:, None] * freq[None, :] % N)
     first = np.concatenate([np.cos(angle), np.sin(angle)], 0)
-    angle = turn * (cells[:, None] * plane[None, :] % N)
+    angle = turn * (paired[:, None] * plane[None, :] % N)
     middle = np.concatenate([np.cos(angle), np.sin(angle)], 0)
     lane_freq = np.zeros(256, np.int64)
     kind = np.full(256, -1)
@@ -53,7 +54,7 @@
     norm = 1.0 / float(N) ** 3
     from_re = (re * cos - im * sin).T * norm
     from_im = (re * sin + im * cos).T * norm
-    angle = turn * (plane[:, None] * cells[None, :] % N)
+    angle = turn * (plane[:, None] * paired[None, :] % N)
     middle_back = np.concatenate([np.cos(angle), np.sin(angle)], 0)
     angle = turn * (freq[:, None] * plane[None, :] % N)
     first_back = np.concatenate([np.cos(angle), np.sin(angle)], 0)
@@ -94,9 +95,22 @@
 
 
 def kernel(
+    index_hbm,
+    coef_hbm,
+    pot_hbm,
+    first_hbm,
+    middle_hbm,
+    to_re_hbm,
+    to_im_hbm,
+    from_re_hbm,
+    from_im_hbm,
+    middle_back_hbm,
+    first_back_hbm,
+    sub_ref,
+    res_ref,
     index_ref,
     coef_ref,
-    pot_ref,
+    pot_flat,
     first,
     middle,
     to_re,
@@ -105,8 +119,10 @@
     from_im,
     middle_back,
     first_back,
-    sub_ref,
-    res_ref,
+    load_sem,
+    pot_rows,
+    pot_ref,
+    field_ref,
     row_key,
     col_key,
     coef_hi,
@@ -117,7 +133,6 @@
     send2,
     recv2,
     trash,
-    table,
     all_coef,
     applied,
     part,
@@ -128,6 +143,25 @@
     band_recv,
     own_sem,
 ):
+    sources = (
+        (index_hbm, index_ref),
+        (coef_hbm, coef_ref),
+        (first_hbm, first),
+        (middle_hbm, middle),
+        (to_re_hbm, to_re),
+        (to_im_hbm, to_im),
+        (pot_hbm, pot_flat),
+        (from_re_hbm, from_re),
+        (from_im_hbm, from_im),
+        (middle_back_hbm, middle_back),
+        (first_back_hbm, first_back),
+    )
+    loads = [
+        pltpu.make_async_copy(src, dst, load_sem.at[k]) for k, (src, dst) in enumerate(sources)
+    ]
+    for load in loads:
+        load.start()
+
     me = lax.axis_index("grid")
     band = lax.axis_index("band")
     sibling = band + 1 - 2 * lax.rem(band, 2)
@@ -145,6 +179,8 @@
     pl.semaphore_signal(barrier, inc=1, device_id={"band": sibling}, device_id_type=MESH)
     pl.semaphore_signal(barrier, inc=1, device_id={"band": across}, device_id_type=MESH)
 
+    loads[0].wait()
+    loads[1].wait()
     cell = index_ref[...].astype(F32)
     line = jnp.floor((cell + 0.5) * (1.0 / N))
     gc = cell - N * line
@@ -176,27 +212,33 @@
             )
         return jnp.concatenate(pieces, 1)
 
-    def scatter_step(i, carry):
-        pieces = []
-        for s in range(KS):
-            row = pl.ds(i * KS + s, 1)
-            mask = iota96h == wide(col_key[row, :])
-            blocks = []
-            for ref in (coef_hi, coef_lo):
-                re = jnp.where(mask, wide(ref[0, row, :]), zero)
-                im = jnp.where(mask, wide(ref[1, row, :]), zero)
-                blocks += [re[:64], im[:64], re[64:], zero32, im[64:], zero32]
-            pieces.append(jnp.concatenate(blocks, 0))
-        acc[...] += lax.dot_general(
-            row_hot(i),
-            jnp.concatenate(pieces, 1),
-            (((1,), (1,)), ((), ())),
-            preferred_element_type=F32,
-        )
-        return carry
+    def scatter_step(low, count):
+        pad = [] if count == 64 else [zero32]
+        iota = iota96h[:count]
+
+        def step(i, carry):
+            pieces = []
+            for s in range(KS):
+                row = pl.ds(i * KS + s, 1)
+                mask = iota == jnp.broadcast_to((col_key[row, :] - low).astype(BF16), (count, 128))
+                blocks = []
+                for ref in (coef_hi, coef_lo):
+                    for k in range(2):
+                        value = jnp.broadcast_to(ref[k, row, :].astype(BF16), (count, 128))
+                        blocks += [jnp.where(mask, value, zero)] + pad
+                pieces.append(jnp.concatenate(blocks, 0))
+            acc[low // 64] += lax.dot_general(
+                row_hot(i),
+                jnp.concatenate(pieces, 1),
+                (((1,), (1,)), ((), ())),
+                preferred_element_type=F32,
+            )
+            return carry
+
+        return step
 
     steps = 128 // KS
-    lax.fori_loop(0, 4, scatter_step, 0)
+    lax.fori_loop(0, steps // 2, scatter_step(0, 64), 0)
     pl.semaphore_wait(barrier, PARTS - 1 + 2)
 
     def band_copy(src, dst, slot, to):
@@ -215,14 +257,14 @@
     to_across.start()
     to_sibling.start()
     keep.start()
-    lax.fori_loop(4, steps, scatter_step, 0)
-
-    def exchange(src, dst, lanes, slot):
+    lax.fori_loop(steps // 2, steps, scatter_step(0, 64), 0)
+
+    def exchange(src, dst, own, lanes, slot):
         def one_copy(i, carry):
             peer = lax.rem(me + i, PARTS)
             pltpu.make_async_remote_copy(
-                src_ref=src.at[:, peer, lanes],
-                dst_ref=dst.at[:, me, lanes],
+                src_ref=src.at[own, peer, lanes],
+                dst_ref=dst.at[own, me, lanes],
                 send_sem=send_sem.at[slot],
                 recv_sem=recv_sem.at[slot],
                 device_id={"grid": peer},
@@ -231,9 +273,11 @@
             return carry
 
         lax.fori_loop(1, PARTS, one_copy, 0)
-        pltpu.make_async_copy(src.at[:, me, lanes], dst.at[:, me, lanes], recv_sem.at[slot]).start()
         pltpu.make_async_copy(
-            src.at[:, me, lanes], trash.at[slot, :, 0, lanes], send_sem.at[slot]
+            src.at[own, me, lanes], dst.at[own, me, lanes], recv_sem.at[slot]
+        ).start()
+        pltpu.make_async_copy(
+            src.at[own, me, lanes], trash.at[own, slot, lanes], send_sem.at[slot]
         ).start()
 
     def arrive(src, dst, lanes, slot):
@@ -244,83 +288,109 @@
 
     lanes_a, lanes_b = pl.ds(0, LA), pl.ds(LA, LB)
 
-    def spectrum(offset):
-        a = [acc[HALF * p : HALF * p + HALF, offset : offset + 128] for p in range(SLAB)]
-        b = [acc[HALF * p : HALF * p + HALF, offset + 128 : offset + 256] for p in range(SLAB)]
-        return (
-            jnp.concatenate(a, 1).astype(BF16),
-            jnp.concatenate([b[0] + pltpu.roll(b[1], 32, 1), b[2]], 1).astype(BF16),
-        )
-
-    hi_a, hi_b = spectrum(0)
-    lo_a, lo_b = spectrum(256)
-    out_a = combine(dot_left(first, hi_a, lo_a), 1.0)
+    every = pl.ds(0, SLAB)
+
+    def spectrum_a(offset):
+        a = [acc[0, HALF * p : HALF * p + HALF, offset : offset + 128] for p in range(SLAB)]
+        return jnp.concatenate(a, 1).astype(BF16)
+
+    def spectrum_b(offset):
+        b = [acc[1, HALF * p : HALF * p + HALF, offset : offset + 128] for p in range(SLAB)]
+        return jnp.concatenate([b[0] + pltpu.roll(b[1], 32, 1), b[2]], 1).astype(BF16)
+
+    loads[2].wait()
+    out = combine(dot_left(first, spectrum_a(0), spectrum_a(128)), 1.0)
     for j in range(SLAB):
-        send1[j, :, 0:LA] = out_a[PARTS * j : PARTS * j + PARTS]
-    exchange(send1, recv1, lanes_a, 0)
-    out_b = combine(dot_left(first, hi_b, lo_b), 1.0)
+        send1[j, :, 0:LA] = out[PARTS * j : PARTS * j + PARTS]
+    exchange(send1, recv1, every, lanes_a, 0)
+    lax.fori_loop(0, steps, scatter_step(64, 32), 0)
+    out = combine(dot_left(first, spectrum_b(0), spectrum_b(128)), 1.0)
     for j in range(SLAB):
-        send1[j, :, LA:LANES] = out_b[PARTS * j : PARTS * j + PARTS]
-    exchange(send1, recv1, lanes_b, 1)
+        send1[j, :, LA:LANES] = out[PARTS * j : PARTS * j + PARTS]
+    exchange(send1, recv1, every, lanes_b, 1)
 
     band_copy(coef_ref, all_coef.at[across], 0, across).wait_recv()
     onward = band_copy(all_coef.at[across], all_coef.at[across], 2, sibling)
     onward.start()
 
+    for load in loads[3:]:
+        load.wait()
+
+    def pot_row(q, carry):
+        both = pot_flat[:, pl.ds(pl.multiple_of(q * 384, 128), 384)]
+        for j in range(SLAB):
+            pot_rows[j, pl.ds(q, 1), :] = both[j : j + 1]
+        return carry
+
+    lax.fori_loop(0, HALF, pot_row, 0)
+    for j in range(SLAB):
+        pot_ref[j, 0:HALF] = pot_rows[j, :, 0:N]
+        pot_ref[j, HALF:N] = pltpu.roll(pot_rows[j], N, 1)[:, 0:N]
+
     arrive(send1, recv1, lanes_a, 0)
+
+    def middle_a(j, carry):
+        x = recv1[j, :, 0:LA]
+        x = jnp.concatenate([x[:, 0:128], x[:, 128:256], x[:, 256:384]], 0)
+        hi, lo = halves(combine(dot_left(middle, *halves(x)), 1.0))
+        field_ref[j, 0] = dot_right(hi, lo, to_re[:, 0:128])
+        field_ref[j, 1] = dot_right(hi, lo, to_im[:, 0:128])
+        return carry
+
+    lax.fori_loop(0, SLAB, middle_a, 0)
     arrive(send1, recv1, lanes_b, 1)
 
-    def middle_step(j, carry):
-        x = recv1[j]
-        a = jnp.concatenate([x[:, 0:128], x[:, 128:256], x[:, 256:384]], 0)
-        b = jnp.concatenate([x[:, 384:512], pltpu.roll(x[:, 384:512], 96, 1), x[:, 512:640]], 0)
-        x = combine(dot_left(middle, *halves(jnp.concatenate([a, b], 1))), 1.0)
-        hi, lo = halves(x)
+    def middle_b(j, carry):
+        x = recv1[j, :, LA:LANES]
+        x = jnp.concatenate([x[:, 0:128], pltpu.roll(x[:, 0:128], 96, 1), x[:, 128:256]], 0)
+        hi, lo = halves(combine(dot_left(middle, *halves(x)), 1.0))
         pot = pot_ref[j]
-        field_re = dot_right(hi, lo, to_re) * pot
-        field_im = dot_right(hi, lo, to_im) * pot
+        field_re = (field_ref[j, 0] + dot_right(hi, lo, to_re[:, 128:256])) * pot
+        field_im = (field_ref[j, 1] + dot_right(hi, lo, to_im[:, 128:256])) * pot
         x = dot_right(*halves(field_re), from_re) + dot_right(*halves(field_im), from_im)
         x = combine(dot_left(middle_back, *halves(x)), -1.0)
         for p in range(SLAB):
             send2[j, :, 128 * p : 128 * p + 128] = x[PARTS * p : PARTS * p + PARTS, 0:128]
         send2[j, :, 384:512] = x[0:64, 128:256] + pltpu.roll(x[64:128, 128:256], 32, 1)
         send2[j, :, 512:640] = x[128:192, 128:256]
+        exchange(send2, recv2, pl.ds(j, 1), lanes_a, 2)
         return carry
 
-    lax.fori_loop(0, SLAB, middle_step, 0)
-    exchange(send2, recv2, lanes_a, 2)
-    exchange(send2, recv2, lanes_b, 3)
+    lax.fori_loop(0, SLAB, middle_b, 0)
+    exchange(send2, recv2, every, lanes_b, 3)
+
+    def gather(low, count):
+        def rows_of(x):
+            if low == 0:
+                return [x[:, 0:128], x[:, 128:256], x[:, 256:384]]
+            return [x[:, 0:128], pltpu.roll(x[:, 0:128], 96, 1), x[:, 128:256]]
+
+        x = recv2[:, :, 0:LA] if low == 0 else recv2[:, :, LA:LANES]
+        x = combine(dot_left(first_back, *halves(x.reshape(N, x.shape[-1]))), -1.0)
+        x = jnp.concatenate(rows_of(x), 0).T
+        hi, lo = halves(jnp.concatenate([x[0:count], x[64 : 64 + count]], 0))
+        table = jnp.concatenate([hi, lo], 0)
+        iota = iota96[:count]
+
+        def step(i, carry):
+            found = dot(table, row_hot(i))
+            found = found[: 2 * count] + found[2 * count :]
+            for s in range(KS):
+                row = pl.ds(i * KS + s, 1)
+                mask = iota == jnp.broadcast_to(col_key[row, :] - low, (count, 128))
+                here = found[:, 128 * s : 128 * s + 128]
+                for k in range(2):
+                    kept = jnp.where(mask, here[count * k : count * k + count], 0.0)
+                    kept = kept.reshape(count // 8, 8, 128).sum(0).sum(0, keepdims=True)
+                    applied[k, row, :] = kept if low == 0 else applied[k, row, :] + kept
+            return carry
+
+        lax.fori_loop(0, steps, step, 0)
+
     arrive(send2, recv2, lanes_a, 2)
+    gather(0, 64)
     arrive(send2, recv2, lanes_b, 3)
-
-    x = recv2[...].reshape(N, LANES)
-    x = combine(dot_left(first_back, *halves(x)), -1.0)
-    b0 = x[:, 384:512]
-    x = jnp.concatenate(
-        [
-            jnp.concatenate([x[:, 0:128], x[:, 128:256], x[:, 256:384]], 0),
-            jnp.concatenate([b0, pltpu.roll(b0, 96, 1), x[:, 512:640]], 0),
-        ],
-        1,
-    ).T
-    x = jnp.concatenate([x[0:64], x[128:160], x[64:128], x[192:224]], 0)
-    hi, lo = halves(x)
-    table[0] = hi
-    table[1] = lo
-
-    def gather_step(i, carry):
-        hot = row_hot(i)
-        found = dot(table[0], hot) + dot(table[1], hot)
-        for s in range(KS):
-            row = pl.ds(i * KS + s, 1)
-            mask = iota96 == jnp.broadcast_to(col_key[row, :], (HALF, 128))
-            here = found[:, 128 * s : 128 * s + 128]
-            for k in range(2):
-                kept = jnp.where(mask, here[HALF * k : HALF * k + HALF], 0.0)
-                applied[k, row, :] = kept.reshape(12, 8, 128).sum(0).sum(0, keepdims=True)
-        return carry
-
-    lax.fori_loop(0, steps, gather_step, 0)
+    gather(64, 32)
 
     band_copy(coef_ref, all_coef.at[sibling], 1, sibling).wait_recv()
     band_copy(coef_ref, all_coef.at[opposite], 2, sibling).wait_recv()
@@ -353,11 +423,12 @@
 
     lax.fori_loop(1, PARTS, share, 0)
     pltpu.make_async_copy(part.at[:, 0], parts_in.at[:, me], recv_sem.at[4]).start()
-    pltpu.make_async_copy(part.at[:, 0], trash.at[4, pl.ds(0, 1), 0, pl.ds(0, 128)], send_sem.at[4]).start()
+    pltpu.make_async_copy(part.at[:, 0], trash.at[pl.ds(0, 1), 4, pl.ds(0, 128)], send_sem.at[4]).start()
     pltpu.make_async_copy(part, parts_in, recv_sem.at[4]).wait()
 
     line = parts_in[0].sum(0, keepdims=True) * (1.0 / (PARTS * 16384))
-    sub_ref[...] = jnp.broadcast_to(line, (8, 128))
+    sub_ref[0] = line[:, 0:4]
+    sub_ref[1] = line[:, 4:8]
     r_re, r_im = h_re, h_im
     for i in range(4):
         s_re = jnp.broadcast_to(line[:, i : i + 1], (128, 128))
@@ -382,28 +453,32 @@
     tables = [jnp.asarray(t) for t in make_tables()]
     coef = coefficients.reshape(2, 128, 128)
     index = index_map.reshape(128, 128)
-    pot = potential.reshape(SLAB, N, N)
+    inputs = (index, coef, potential, *tables)
     field = VMEM((SLAB, PARTS, LANES), F32)
     sub, res = pl.pallas_call(
         kernel,
         out_shape=(
-            jax.ShapeDtypeStruct((8, 128), F32),
+            jax.ShapeDtypeStruct((2, 1, 4), F32),
             jax.ShapeDtypeStruct((2, 128, 128), F32),
         ),
-        in_specs=[pl.BlockSpec(memory_space=VMEM)] * (3 + len(tables)),
+        in_specs=[pl.BlockSpec(memory_space=pltpu.HBM)] * len(inputs),
         out_specs=[pl.BlockSpec(memory_space=VMEM)] * 2,
-        scratch_shapes=[
+        scratch_shapes=[VMEM(x.shape, x.dtype) for x in inputs]
+        + [
+            pltpu.SemaphoreType.DMA((len(inputs),)),
+            VMEM((SLAB, HALF, 384), F32),
+            VMEM((SLAB, N, N), F32),
+            VMEM((SLAB, 2, N, N), F32),
             VMEM((128, 128), F32),
             VMEM((128, 128), F32),
             VMEM((2, 128, 128), F32),
             VMEM((2, 128, 128), F32),
-            VMEM((SLAB * HALF, 512), F32),
+            VMEM((2, SLAB * HALF, 256), F32),
             field,
             field,
             field,
             field,
-            VMEM((5, SLAB, 1, LANES), F32),
-            VMEM((2, N, SLAB * HALF), BF16),
+            VMEM((SLAB, 8, LANES), F32),
             VMEM((4, 2, 128, 128), F32),
             VMEM((2, 128, 128), F32),
             VMEM((1, PARTS, 128), F32),
@@ -415,11 +490,11 @@
             pltpu.SemaphoreType.DMA,
         ],
         compiler_params=pltpu.CompilerParams(
-            collective_id=0, has_side_effects=True, vmem_limit_bytes=48 << 20
+            collective_id=0, has_side_effects=True, vmem_limit_bytes=56 << 20
         ),
         name="apply_potential",
-    )(index, coef, pot, *tables)
-    return sub[0, :8].reshape(2, 4, 1), res.reshape(2, 1, 16384)
+    )(*inputs)
+    return sub.transpose(0, 2, 1), res.reshape(2, 1, 16384)
 
 
 def solution(mesh):

time: 75.3 us -> 66.5 us (0.88)
  local copies, waits for them, and re-layouts: 8.35 us -> 2.78 us
  Pallas kernels: 65.8 us -> 63 us
    unnamed x21 -> x4, local copies, waits for them, and re-layouts: 6.17 us -> 2.78 us
    pallas_call x1, Pallas kernels: 65.8 us -> 63 us  [local(): pl.pallas_call(kernel, out_shape=(jax.ShapeDtypeStruct((2, 1, 4), F32), j...]
    reshape x1 -> x0, local copies, waits for them, and re-layouts: 1.51 us -> none  [local(): pot = potential.reshape(SLAB, N, N)]
where the time goes in v2:
time: 66.5 us; the launch traced here: 66.4 us
  Pallas kernels  63 us (95%)
  local copies, waits for them, and re-layouts  2.78 us (4%)
    pallas_call x1, Pallas kernels, local(): pl.pallas_call(kernel, out_shape=(jax.ShapeDtypeStruct((2, 1, 4), F32), j...  63 us
    unnamed x4, local copies, waits for them, and re-layouts  2.78 us

profile of v2, /device:TPU:8, one launch (start us, length us, event | category | flops | bytes accessed | tf_op | source)
XLA Modules:
  0.0 66.4 jit_solution(2171573967555020584)
XLA Ops:
  0.6 63.0 %apply_potential.1 = (f32[2,1,4]{2,1,0:T(1,128)}, f32[2,128,128]{2,1,0:T(8,128)}) custom-call(s32[128,128]{1,0:T(8,128)} %bitcast.8, f32[2,128,128]{2,1,0:T(8,128)} %bitcast.6, f32[3,36864]{1,0:T(4,128)} %pot_hbm.1, bf16[2,384,96]{2,1,0:T(8,128)(2,1)} %constant.16.clone.first_hbm, bf16[2,384,192]{2,1,0:T(8,128)(2,1)} %constant.17.clone.middle_hbm, ...), custom_call_target="tpu_custom_call" | custom-call | tf_op jit(solution)/shard_map/apply_potential/pallas_call | solution.py:458
  63.6 0.0 copy-start
  63.6 0.6 copy-done
  64.3 0.6 copy.17
  64.8 1.6 %copy.18 = f32[2,1,16384]{2,1,0:T(1,128)} copy(f32[2,1,16384]{2,1,0:T(1,128)} %bitcast.7) | data formatting | bytes 262144
Async XLA Ops:
  63.6 0.7 copy-start

commit v3 on v2

--- a/solution.py
+++ b/solution.py
@@ -14,7 +14,7 @@
 HALF = 96
 PARTS = 64
 SLAB = 3
-KS = 16
+KS = 32
 LA, LB = 384, 256
 LANES = LA + LB
 F32, BF16 = jnp.float32, jnp.bfloat16
@@ -40,12 +40,16 @@
     first = np.concatenate([np.cos(angle), np.sin(angle)], 0)
     angle = turn * (paired[:, None] * plane[None, :] % N)
     middle = np.concatenate([np.cos(angle), np.sin(angle)], 0)
+    column = np.arange(HALF)
+    column = np.where(column < 32, column, np.where(column < 64, column + 16, column))
+    column[64:80] = np.arange(32, 48)
+    col_freq = freq[column]
     lane_freq = np.zeros(256, np.int64)
     kind = np.full(256, -1)
-    lane_freq[0:64], kind[0:64] = freq[:64], 0
-    lane_freq[64:128], kind[64:128] = freq[:64], 1
-    lane_freq[128:160], kind[128:160] = freq[64:], 0
-    lane_freq[192:224], kind[192:224] = freq[64:], 1
+    lane_freq[0:64], kind[0:64] = col_freq[:64], 0
+    lane_freq[64:128], kind[64:128] = col_freq[:64], 1
+    lane_freq[128:160], kind[128:160] = col_freq[64:], 0
+    lane_freq[192:224], kind[192:224] = col_freq[64:], 1
     angle = turn * (lane_freq[:, None] * cells[None, :] % N)
     cos, sin = np.cos(angle), np.sin(angle)
     re, im = (kind == 0)[:, None], (kind == 1)[:, None]
@@ -59,7 +63,20 @@
     angle = turn * (freq[:, None] * plane[None, :] % N)
     first_back = np.concatenate([np.cos(angle), np.sin(angle)], 0)
     tables = (first, middle, to_re, to_im, from_re, from_im, middle_back, first_back)
-    return [np.stack(split(table)) for table in tables]
+    signed = np.where(fold < HALF // 2, fold, fold - HALF)
+    moved = np.abs(signed) > 42
+    home = np.where(moved, np.sign(signed) * (85 - np.abs(signed)), signed) % 85
+    select = np.zeros((2, SLAB, HALF, 256), np.float32)
+    for p in range(SLAB):
+        for f in range(HALF):
+            if f != HALF // 2:
+                select[int(moved[f]), p, f, 85 * p + home[f]] = 1.0
+    select = select.reshape(2, SLAB * HALF, 256).astype(ml_dtypes.bfloat16)
+    row_fa = np.arange(256) % 85
+    row_fa = np.where(row_fa < 43, row_fa, row_fa - 85)
+    col_fc = signed[column]
+    inside = row_fa[None, :] ** 2 + col_fc[:, None] ** 2 < (N // 4) ** 2
+    return [np.stack(split(table)) for table in tables] + [select, inside.astype(np.float32)]
 
 
 def halves(x):
@@ -106,6 +123,8 @@
     from_im_hbm,
     middle_back_hbm,
     first_back_hbm,
+    select_hbm,
+    inside_hbm,
     sub_ref,
     res_ref,
     index_ref,
@@ -119,12 +138,16 @@
     from_im,
     middle_back,
     first_back,
+    select,
+    inside,
     load_sem,
     pot_rows,
     pot_ref,
     field_ref,
     row_key,
     col_key,
+    row_home,
+    col_home,
     coef_hi,
     coef_lo,
     acc,
@@ -155,6 +178,8 @@
         (from_im_hbm, from_im),
         (middle_back_hbm, middle_back),
         (first_back_hbm, first_back),
+        (select_hbm, select),
+        (inside_hbm, inside),
     )
     loads = [
         pltpu.make_async_copy(src, dst, load_sem.at[k]) for k, (src, dst) in enumerate(sources)
@@ -170,13 +195,17 @@
 
     barrier = pltpu.get_barrier_semaphore()
 
-    def greet(i, carry):
-        peer = lax.rem(me + i, PARTS)
-        pl.semaphore_signal(barrier, inc=1, device_id={"grid": peer}, device_id_type=MESH)
-        return carry
-
-    lax.fori_loop(1, PARTS, greet, 0)
-    pl.semaphore_signal(barrier, inc=1, device_id={"band": sibling}, device_id_type=MESH)
+    def greet(i):
+        pl.semaphore_signal(
+            barrier,
+            inc=1,
+            device_id={
+                "grid": lax.rem(me + i, PARTS),
+                "band": jnp.where(i == 0, sibling, band),
+            },
+            device_id_type=MESH,
+        )
+
     pl.semaphore_signal(barrier, inc=1, device_id={"band": across}, device_id_type=MESH)
 
     loads[0].wait()
@@ -187,7 +216,20 @@
     ga = jnp.floor((cell + 0.5) * (1.0 / (SLAB * N)))
     slab = line - SLAB * ga
     row_key[...] = slab * HALF + jnp.where(ga < HALF, ga, ga - HALF)
-    col_key[...] = jnp.where(gc < HALF, gc, gc - HALF)
+    fold = jnp.where(gc < HALF, gc, gc - HALF)
+    col = jnp.where(fold < 32, fold, jnp.where(fold < 80, fold - 16, fold))
+    col = jnp.where(jnp.logical_and(fold >= 32, fold < 48), fold + 32, col)
+    col_key[...] = col
+    fa = jnp.where(ga < HALF, ga, ga - N)
+    moved = jnp.abs(fa) > 42
+    home = jnp.where(moved, jnp.where(fa > 0, 85 - fa, -85 - fa), fa)
+    row_home[...] = slab * 85 + jnp.where(home < 0, home + 85, home)
+    turned = jnp.where(
+        col < 64,
+        jnp.where(col < 32, col + 32, col - 32),
+        jnp.where(col < 80, col + 16, col - 16),
+    )
+    col_home[...] = jnp.where(moved, turned, col)
     coef = coef_ref[...]
     coef_hi[...] = coef.astype(BF16).astype(F32)
     coef_lo[...] = coef - coef.astype(BF16).astype(F32)
@@ -210,6 +252,15 @@
                     [jnp.where(iota96h == wide(key - HALF * p), one, zero) for p in range(SLAB)], 0
                 )
             )
+        return jnp.concatenate(pieces, 1)
+
+    iota256h = lax.broadcasted_iota(jnp.int32, (256, 128), 0).astype(F32).astype(BF16)
+
+    def home_hot(i):
+        pieces = []
+        for s in range(KS):
+            key = row_home[pl.ds(i * KS + s, 1), :].astype(BF16)
+            pieces.append(jnp.where(iota256h == jnp.broadcast_to(key, (256, 128)), one, zero))
         return jnp.concatenate(pieces, 1)
 
     def scatter_step(low, count):
@@ -238,7 +289,14 @@
         return step
 
     steps = 128 // KS
-    lax.fori_loop(0, steps // 2, scatter_step(0, 64), 0)
+    early = scatter_step(0, 64)
+
+    def early_step(i, carry):
+        for k in range(2 * PARTS // steps):
+            greet(i * (2 * PARTS // steps) + k)
+        return early(i, carry)
+
+    lax.fori_loop(0, steps // 2, early_step, 0)
     pl.semaphore_wait(barrier, PARTS - 1 + 2)
 
     def band_copy(src, dst, slot, to):
@@ -370,14 +428,24 @@
         x = jnp.concatenate(rows_of(x), 0).T
         hi, lo = halves(jnp.concatenate([x[0:count], x[64 : 64 + count]], 0))
         table = jnp.concatenate([hi, lo], 0)
+        turned = []
+        for k in range(4):
+            block = table[count * k : count * k + count]
+            turned += [block[count // 2 :], block[: count // 2]]
+        keep_own = inside[low : low + count, :]
+        table = jnp.where(
+            jnp.concatenate([keep_own] * 4, 0) > 0.5,
+            dot(table, select[0]),
+            dot(jnp.concatenate(turned, 0), select[1]),
+        ).astype(BF16)
         iota = iota96[:count]
 
         def step(i, carry):
-            found = dot(table, row_hot(i))
+            found = dot(table, home_hot(i))
             found = found[: 2 * count] + found[2 * count :]
             for s in range(KS):
                 row = pl.ds(i * KS + s, 1)
-                mask = iota == jnp.broadcast_to(col_key[row, :] - low, (count, 128))
+                mask = iota == jnp.broadcast_to(col_home[row, :] - low, (count, 128))
                 here = found[:, 128 * s : 128 * s + 128]
                 for k in range(2):
                     kept = jnp.where(mask, here[count * k : count * k + count], 0.0)
@@ -469,6 +537,8 @@
             VMEM((SLAB, HALF, 384), F32),
             VMEM((SLAB, N, N), F32),
             VMEM((SLAB, 2, N, N), F32),
+            VMEM((128, 128), F32),
+            VMEM((128, 128), F32),
             VMEM((128, 128), F32),
             VMEM((128, 128), F32),
             VMEM((2, 128, 128), F32),

time: 66.5 us -> 61.9 us (0.931)
  Pallas kernels: 63 us -> 58.2 us
    pallas_call x1, Pallas kernels: 63 us -> 58.2 us  [local(): pl.pallas_call(kernel, out_shape=(jax.ShapeDtypeStruct((2, 1, 4), F32), j...]
where the time goes in v3:
time: 61.9 us; the launch traced here: 61.6 us
  Pallas kernels  58.2 us (94%)
  local copies, waits for them, and re-layouts  2.78 us (4%)
  between operations  0.65 us (1%)
    pallas_call x1, Pallas kernels, local(): pl.pallas_call(kernel, out_shape=(jax.ShapeDtypeStruct((2, 1, 4), F32), j...  58.2 us
    unnamed x4, local copies, waits for them, and re-layouts  2.78 us

profile of v3, /device:TPU:8, one launch (start us, length us, event | category | flops | bytes accessed | tf_op | source)
XLA Modules:
  0.0 61.6 jit_solution(12965537099314648936)
XLA Ops:
  0.6 58.2 %apply_potential.1 = (f32[2,1,4]{2,1,0:T(1,128)}, f32[2,128,128]{2,1,0:T(8,128)}) custom-call(s32[128,128]{1,0:T(8,128)} %bitcast.8, f32[2,128,128]{2,1,0:T(8,128)} %bitcast.6, f32[3,36864]{1,0:T(4,128)} %pot_hbm.1, bf16[2,384,96]{2,1,0:T(8,128)(2,1)} %constant.20.clone.first_hbm, bf16[2,384,192]{2,1,0:T(8,128)(2,1)} %constant.21.clone.middle_hbm, ...), custom_call_target="tpu_custom_call" | custom-call | tf_op jit(solution)/shard_map/apply_potential/pallas_call | solution.py:526
  58.8 0.0 copy-start
  58.8 0.6 %copy-done = f32[2,1,4]{2,1,0:T(1,128)S(1)} copy-done((f32[2,1,4]{2,1,0:T(1,128)S(1)}, f32[2,1,4]{2,1,0:T(1,128)}, u32[]{:S(2)}) %copy-start) | copy-done | bytes 56
  59.5 0.6 copy.19
  60.0 1.6 %copy.20 = f32[2,1,16384]{2,1,0:T(1,128)} copy(f32[2,1,16384]{2,1,0:T(1,128)} %bitcast.7) | data formatting | bytes 262144
Async XLA Ops:
  58.8 0.7 %copy-start = (f32[2,1,4]{2,1,0:T(1,128)S(1)}, f32[2,1,4]{2,1,0:T(1,128)}, u32[]{:S(2)}) copy-start(f32[2,1,4]{2,1,0:T(1,128)} %get-tuple-element.4) | copy-start | bytes 100

commit v4 on v3

--- a/solution.py
+++ b/solution.py
@@ -14,7 +14,7 @@
 HALF = 96
 PARTS = 64
 SLAB = 3
-KS = 32
+KS = 64
 LA, LB = 384, 256
 LANES = LA + LB
 F32, BF16 = jnp.float32, jnp.bfloat16
@@ -156,6 +156,7 @@
     send2,
     recv2,
     trash,
+    last_plane,
     all_coef,
     applied,
     part,
@@ -309,10 +310,15 @@
             device_id_type=MESH,
         )
 
-    to_across = band_copy(coef_ref, all_coef.at[band], 0, across)
-    to_sibling = band_copy(coef_ref, all_coef.at[band], 1, sibling)
+    def to_across(k):
+        return band_copy(coef_ref.at[k], all_coef.at[band, k], k, across)
+
+    def onward(k):
+        return band_copy(all_coef.at[across, k], all_coef.at[across, k], 3 + k, sibling)
+
+    to_sibling = band_copy(coef_ref, all_coef.at[band], 2, sibling)
     keep = pltpu.make_async_copy(coef_ref, all_coef.at[band], own_sem)
-    to_across.start()
+    to_across(0).start()
     to_sibling.start()
     keep.start()
     lax.fori_loop(steps // 2, steps, scatter_step(0, 64), 0)
@@ -338,15 +344,18 @@
             src.at[own, me, lanes], trash.at[own, slot, lanes], send_sem.at[slot]
         ).start()
 
-    def arrive(src, dst, lanes, slot):
-        pltpu.make_async_copy(src.at[:, :, lanes], dst.at[:, :, lanes], recv_sem.at[slot]).wait()
-
-    def sent(src, dst, lanes, slot):
-        pltpu.make_async_copy(src.at[:, :, lanes], dst.at[:, :, lanes], send_sem.at[slot]).wait()
-
-    lanes_a, lanes_b = pl.ds(0, LA), pl.ds(LA, LB)
-
-    every = pl.ds(0, SLAB)
+    def arrive(src, dst, lanes, slot, own=pl.ds(0, SLAB)):
+        pltpu.make_async_copy(
+            src.at[own, :, lanes], dst.at[own, :, lanes], recv_sem.at[slot]
+        ).wait()
+
+    def sent(src, dst, lanes, slot, own=pl.ds(0, SLAB)):
+        pltpu.make_async_copy(
+            src.at[own, :, lanes], dst.at[own, :, lanes], send_sem.at[slot]
+        ).wait()
+
+    lanes_a, lanes_b, lanes_c = pl.ds(0, LA), pl.ds(LA, 128), pl.ds(LA + 128, 128)
+    every, two = pl.ds(0, SLAB), pl.ds(0, 2)
 
     def spectrum_a(offset):
         a = [acc[0, HALF * p : HALF * p + HALF, offset : offset + 128] for p in range(SLAB)]
@@ -364,12 +373,14 @@
     lax.fori_loop(0, steps, scatter_step(64, 32), 0)
     out = combine(dot_left(first, spectrum_b(0), spectrum_b(128)), 1.0)
     for j in range(SLAB):
-        send1[j, :, LA:LANES] = out[PARTS * j : PARTS * j + PARTS]
+        send1[j, :, LA : LA + 128] = out[PARTS * j : PARTS * j + PARTS, 0:128]
+    send1[0, :, 512:640] = out[0:64, 128:256] + pltpu.roll(out[64:128, 128:256], 32, 1)
+    send1[1, :, 512:640] = out[128:192, 128:256]
     exchange(send1, recv1, every, lanes_b, 1)
-
-    band_copy(coef_ref, all_coef.at[across], 0, across).wait_recv()
-    onward = band_copy(all_coef.at[across], all_coef.at[across], 2, sibling)
-    onward.start()
+    exchange(send1, recv1, two, lanes_c, 5)
+
+    band_copy(coef_ref.at[0], all_coef.at[across, 0], 0, across).wait_recv()
+    onward(0).start()
 
     for load in loads[3:]:
         load.wait()
@@ -397,10 +408,13 @@
 
     lax.fori_loop(0, SLAB, middle_a, 0)
     arrive(send1, recv1, lanes_b, 1)
+    arrive(send1, recv1, lanes_c, 5, two)
 
     def middle_b(j, carry):
-        x = recv1[j, :, LA:LANES]
-        x = jnp.concatenate([x[:, 0:128], pltpu.roll(x[:, 0:128], 96, 1), x[:, 128:256]], 0)
+        x = recv1[j, :, LA : LA + 128]
+        y = recv1[j // 2, :, 512:640]
+        y = jnp.where(j == 1, pltpu.roll(y, 96, 1), y)
+        x = jnp.concatenate([x, pltpu.roll(x, 96, 1), y], 0)
         hi, lo = halves(combine(dot_left(middle, *halves(x)), 1.0))
         pot = pot_ref[j]
         field_re = (field_ref[j, 0] + dot_right(hi, lo, to_re[:, 128:256])) * pot
@@ -410,12 +424,16 @@
         for p in range(SLAB):
             send2[j, :, 128 * p : 128 * p + 128] = x[PARTS * p : PARTS * p + PARTS, 0:128]
         send2[j, :, 384:512] = x[0:64, 128:256] + pltpu.roll(x[64:128, 128:256], 32, 1)
-        send2[j, :, 512:640] = x[128:192, 128:256]
+        last_plane[j] = x[128:192, 128:256]
         exchange(send2, recv2, pl.ds(j, 1), lanes_a, 2)
         return carry
 
+    to_across(1).start()
     lax.fori_loop(0, SLAB, middle_b, 0)
     exchange(send2, recv2, every, lanes_b, 3)
+    send2[0, :, 512:640] = last_plane[0] + pltpu.roll(last_plane[1], 32, 1)
+    send2[1, :, 512:640] = last_plane[2]
+    exchange(send2, recv2, two, lanes_c, 6)
 
     def gather(low, count):
         def rows_of(x):
@@ -423,8 +441,13 @@
                 return [x[:, 0:128], x[:, 128:256], x[:, 256:384]]
             return [x[:, 0:128], pltpu.roll(x[:, 0:128], 96, 1), x[:, 128:256]]
 
-        x = recv2[:, :, 0:LA] if low == 0 else recv2[:, :, LA:LANES]
-        x = combine(dot_left(first_back, *halves(x.reshape(N, x.shape[-1]))), -1.0)
+        if low == 0:
+            x = recv2[:, :, 0:LA].reshape(N, LA)
+        else:
+            y = recv2[0, :, 512:640]
+            y = jnp.concatenate([y, pltpu.roll(y, 96, 1), recv2[1, :, 512:640]], 0)
+            x = jnp.concatenate([recv2[:, :, LA : LA + 128].reshape(N, 128), y], 1)
+        x = combine(dot_left(first_back, *halves(x)), -1.0)
         x = jnp.concatenate(rows_of(x), 0).T
         hi, lo = halves(jnp.concatenate([x[0:count], x[64 : 64 + count]], 0))
         table = jnp.concatenate([hi, lo], 0)
@@ -455,13 +478,17 @@
 
         lax.fori_loop(0, steps, step, 0)
 
+    band_copy(coef_ref.at[1], all_coef.at[across, 1], 1, across).wait_recv()
+    onward(1).start()
     arrive(send2, recv2, lanes_a, 2)
     gather(0, 64)
     arrive(send2, recv2, lanes_b, 3)
+    arrive(send2, recv2, lanes_c, 6, two)
     gather(64, 32)
 
-    band_copy(coef_ref, all_coef.at[sibling], 1, sibling).wait_recv()
-    band_copy(coef_ref, all_coef.at[opposite], 2, sibling).wait_recv()
+    band_copy(coef_ref, all_coef.at[sibling], 2, sibling).wait_recv()
+    for k in range(2):
+        band_copy(coef_ref.at[k], all_coef.at[opposite, k], 3 + k, sibling).wait_recv()
     keep.wait()
 
     h_re, h_im = applied[0], applied[1]
@@ -509,12 +536,20 @@
 
     sent(send1, recv1, lanes_a, 0)
     sent(send1, recv1, lanes_b, 1)
+    sent(send1, recv1, lanes_c, 5, two)
     sent(send2, recv2, lanes_a, 2)
     sent(send2, recv2, lanes_b, 3)
+    sent(send2, recv2, lanes_c, 6, two)
     pltpu.make_async_copy(part, parts_in, send_sem.at[4]).wait()
-    to_across.wait_send()
     to_sibling.wait_send()
-    onward.wait_send()
+    for k in range(2):
+        to_across(k).wait_send()
+        onward(k).wait_send()
+
+
+def hand_over(sub_in, res_in, sub_out, res_out):
+    sub_out[...] = sub_in[...]
+    res_out[...] = res_in[...]
 
 
 def local(coefficients, index_map, potential):
@@ -549,14 +584,15 @@
             field,
             field,
             VMEM((SLAB, 8, LANES), F32),
+            VMEM((SLAB, PARTS, 128), F32),
             VMEM((4, 2, 128, 128), F32),
             VMEM((2, 128, 128), F32),
             VMEM((1, PARTS, 128), F32),
             VMEM((1, PARTS, 128), F32),
+            pltpu.SemaphoreType.DMA((7,)),
+            pltpu.SemaphoreType.DMA((7,)),
             pltpu.SemaphoreType.DMA((5,)),
             pltpu.SemaphoreType.DMA((5,)),
-            pltpu.SemaphoreType.DMA((3,)),
-            pltpu.SemaphoreType.DMA((3,)),
             pltpu.SemaphoreType.DMA,
         ],
         compiler_params=pltpu.CompilerParams(
@@ -564,6 +600,16 @@
         ),
         name="apply_potential",
     )(*inputs)
+    sub, res = pl.pallas_call(
+        hand_over,
+        out_shape=(
+            jax.ShapeDtypeStruct((2, 1, 4), F32),
+            jax.ShapeDtypeStruct((2, 128, 128), F32),
+        ),
+        in_specs=[pl.BlockSpec(memory_space=VMEM), pl.BlockSpec(memory_space=VMEM)],
+        out_specs=[pl.BlockSpec(memory_space=VMEM), pl.BlockSpec(memory_space=VMEM)],
+        name="hand_over",
+    )(sub, res)
     return sub.transpose(0, 2, 1), res.reshape(2, 1, 16384)
 
 

time: 61.9 us -> 58.6 us (0.947)
  local copies, waits for them, and re-layouts: 2.78 us -> 0 us
    unnamed x4 -> x0, local copies, waits for them, and re-layouts: 2.78 us -> none
    pallas_call x1, Pallas kernels: 58.2 us -> 56 us  [local(): pl.pallas_call(kernel, out_shape=(jax.ShapeDtypeStruct((2, 1, 4), F32), j...]
    pallas_call x0 -> x1, Pallas kernels: none -> 1.58 us  [local(): pl.pallas_call(hand_over, out_shape=(jax.ShapeDtypeStruct((2, 1, 4), F32)...]
where the time goes in v4:
time: 58.6 us; the launch traced here: 58.2 us
  Pallas kernels  57.6 us (98%)
  between operations  0.64 us (1%)
    pallas_call x1, Pallas kernels, local(): pl.pallas_call(kernel, out_shape=(jax.ShapeDtypeStruct((2, 1, 4), F32), j...  56 us
    pallas_call x1, Pallas kernels, local(): pl.pallas_call(hand_over, out_shape=(jax.ShapeDtypeStruct((2, 1, 4), F32)...  1.58 us

profile of v4, /device:TPU:8, one launch (start us, length us, event | category | flops | bytes accessed | tf_op | source)
XLA Modules:
  0.0 58.2 jit_solution(13226420340425199501)
XLA Ops:
  0.6 56.0 %apply_potential.1 = (f32[2,1,4]{2,1,0:T(1,128)}, f32[2,128,128]{2,1,0:T(8,128)}) custom-call(s32[128,128]{1,0:T(8,128)} %bitcast.7, f32[2,128,128]{2,1,0:T(8,128)} %bitcast.6, f32[3,36864]{1,0:T(4,128)} %pot_hbm.1, bf16[2,384,96]{2,1,0:T(8,128)(2,1)} %constant.20.clone.first_hbm, bf16[2,384,192]{2,1,0:T(8,128)(2,1)} %constant.21.clone.middle_hbm, ...), custom_call_target="tpu_custom_call" | custom-call | tf_op jit(solution)/shard_map/apply_potential/pallas_call | solution.py:561
  56.6 1.6 %hand_over.1 = (f32[2,1,4]{2,1,0:T(1,128)}, f32[2,128,128]{2,1,0:T(8,128)}) custom-call(f32[2,1,4]{2,1,0:T(1,128)} %get-tuple-element.6.sub_in, f32[2,128,128]{2,1,0:T(8,128)} %get-tuple-element.7.res_in), custom_call_target="tpu_custom_call" | custom-call | tf_op jit(solution)/shard_map/hand_over/pallas_call | solution.py:603

commit v5 on v4

--- a/solution.py
+++ b/solution.py
@@ -15,6 +15,7 @@
 PARTS = 64
 SLAB = 3
 KS = 64
+KG = 128
 LA, LB = 384, 256
 LANES = LA + LB
 F32, BF16 = jnp.float32, jnp.bfloat16
@@ -259,8 +260,8 @@
 
     def home_hot(i):
         pieces = []
-        for s in range(KS):
-            key = row_home[pl.ds(i * KS + s, 1), :].astype(BF16)
+        for s in range(KG):
+            key = row_home[pl.ds(i * KG + s, 1), :].astype(BF16)
             pieces.append(jnp.where(iota256h == jnp.broadcast_to(key, (256, 128)), one, zero))
         return jnp.concatenate(pieces, 1)
 
@@ -466,8 +467,8 @@
         def step(i, carry):
             found = dot(table, home_hot(i))
             found = found[: 2 * count] + found[2 * count :]
-            for s in range(KS):
-                row = pl.ds(i * KS + s, 1)
+            for s in range(KG):
+                row = pl.ds(i * KG + s, 1)
                 mask = iota == jnp.broadcast_to(col_home[row, :] - low, (count, 128))
                 here = found[:, 128 * s : 128 * s + 128]
                 for k in range(2):
@@ -476,7 +477,7 @@
                     applied[k, row, :] = kept if low == 0 else applied[k, row, :] + kept
             return carry
 
-        lax.fori_loop(0, steps, step, 0)
+        lax.fori_loop(0, 128 // KG, step, 0)
 
     band_copy(coef_ref.at[1], all_coef.at[across, 1], 1, across).wait_recv()
     onward(1).start()

time: 58.6 us -> 58.2 us (level)
  no operation moved by 1% of the time
where the time goes in v5:
time: 58.2 us; the launch traced here: 57.8 us
  Pallas kernels  57.2 us (98%)
  between operations  0.64 us (1%)
    pallas_call x1, Pallas kernels, local(): pl.pallas_call(kernel, out_shape=(jax.ShapeDtypeStruct((2, 1, 4), F32), j...  55.6 us
    pallas_call x1, Pallas kernels, local(): pl.pallas_call(hand_over, out_shape=(jax.ShapeDtypeStruct((2, 1, 4), F32)...  1.58 us

profile of v5, /device:TPU:8, one launch (start us, length us, event | category | flops | bytes accessed | tf_op | source)
XLA Modules:
  0.0 57.8 jit_solution(6647317242293358322)
XLA Ops:
  0.6 55.6 %apply_potential.1 = (f32[2,1,4]{2,1,0:T(1,128)}, f32[2,128,128]{2,1,0:T(8,128)}) custom-call(s32[128,128]{1,0:T(8,128)} %bitcast.7, f32[2,128,128]{2,1,0:T(8,128)} %bitcast.6, f32[3,36864]{1,0:T(4,128)} %pot_hbm.1, bf16[2,384,96]{2,1,0:T(8,128)(2,1)} %constant.20.clone.first_hbm, bf16[2,384,192]{2,1,0:T(8,128)(2,1)} %constant.21.clone.middle_hbm, ...), custom_call_target="tpu_custom_call" | custom-call | tf_op jit(solution)/shard_map/apply_potential/pallas_call | solution.py:562
  56.2 1.6 %hand_over.1 = (f32[2,1,4]{2,1,0:T(1,128)}, f32[2,128,128]{2,1,0:T(8,128)}) custom-call(f32[2,1,4]{2,1,0:T(1,128)} %get-tuple-element.6.sub_in, f32[2,128,128]{2,1,0:T(8,128)} %get-tuple-element.7.res_in), custom_call_target="tpu_custom_call" | custom-call | tf_op jit(solution)/shard_map/hand_over/pallas_call | solution.py:604
